TPU v7x, 32 devices: a whole 2x2x4 slice. The times are simulated.
32 devices in a mesh: half: 2 (over y), gx: 4 (over x, core), yz: 4 (over z).
Axes of the slice: x: 2, y: 2, z: 4, core: 2. Of those that a mesh axis runs over, the one named last changes fastest.
Arguments:
- fields: float32 [2, 256, 256, 128], P('half', 'gx', 'yz'), may hold values from -6 to 6
- forcing: float32 [256, 256, 128], P('gx', 'yz'), may hold values from -6 to 6
- step_index: int32 [1], replicated, may hold values from 0 to 63
Outputs:
- fields_out: float32 [2, 256, 256, 128], P('half', 'gx', 'yz')
All inputs are finite; a program needn't handle non-finite values.
Results may differ from a plain program's by a relative error of at most 0.0001.
Values sent between devices are 32-bit elements; how exact they have to be, the bound alone decides.
A program may use at most 128 MiB of HBM per device.

v0:
```python
import math

import jax
import jax.numpy as jnp
from jax import lax
from jax.sharding import PartitionSpec as P

ITERS = 4


def padded_2(value, sides, width):
    for axis, dim in sides:
        size, length = (lax.axis_size(axis), value.shape[dim])
        up = [(i, (i + 1) % size) for i in range(size - 1)]
        down = [(j, i) for i, j in up]
        last = lax.slice_in_dim(value, length - width, length, axis=dim)
        leading = lax.slice_in_dim(value, 0, width, axis=dim)
        before = lax.ppermute(last, axis, up)
        after = lax.ppermute(leading, axis, down)
        value = jnp.concatenate([before, value, after], axis=dim)
    return value


def from_behind(value, axis, steps):
    count = lax.axis_size(axis)
    leading, last = (max(0, -steps), min(count, count - steps))
    return lax.ppermute(value, axis, [(source, source + steps) for source in range(leading, last)])


def widen(rimmed):
    return jnp.pad(rimmed, ((0, 0), (0, 0), (0, 0), (1, 1)))


def inner(padded):
    return padded[:, 1:-1, 1:-1, 1:-1]


def along_x(padded):
    return 0.5 * (padded[:, 2:, 1:-1, 1:-1] - padded[:, :-2, 1:-1, 1:-1])


def laplace(padded):
    total = padded[:, 2:, 1:-1, 1:-1] + padded[:, :-2, 1:-1, 1:-1]
    total = total + padded[:, 1:-1, 2:, 1:-1] + padded[:, 1:-1, :-2, 1:-1]
    total = total + padded[:, 1:-1, 1:-1, 2:] + padded[:, 1:-1, 1:-1, :-2]
    return total - 6.0 * inner(padded)


def update(field, padded, forcing, phase):
    return field + 0.2 * (
        -field * along_x(padded) + 0.5 * laplace(padded) + forcing * jnp.sin(phase)
    )


def advance(field, forcing, phase):
    rimmed = padded_2(field, (("gx", 1), ("yz", 2)), 1)
    return (update(field, widen(rimmed), forcing, phase), rimmed)


def retreat(adjoint, padded_base, padded_adj):
    return adjoint + 0.2 * (
        -adjoint * along_x(padded_base)
        + along_x(padded_base * padded_adj)
        + 0.5 * laplace(padded_adj)
    )


def on_device(fields, forcing, step_index):
    omega = 2.0 * math.pi / 64.0
    side = lax.axis_index("half")
    shaped = forcing[None]
    state = fields
    plain_states = []
    rimmed_states = []
    for step in range(ITERS):
        phase = (step_index[0] + step).astype(jnp.float32) * omega
        plain_states.append(state)
        state, rimmed = advance(state, shaped, phase)
        rimmed_states.append(rimmed)
    chosen = jnp.stack(plain_states)
    moved = from_behind(chosen, "half", 1)
    plain_states = [moved[step] for step in range(ITERS)]
    adjoint = fields
    for step in reversed(range(ITERS)):
        rimmed_adj, rimmed_base = (
            padded_2(adjoint, (("gx", 1), ("yz", 2)), 1),
            padded_2(plain_states[step], (("gx", 1), ("yz", 2)), 1),
        )
        adjoint = retreat(adjoint, widen(rimmed_base), widen(rimmed_adj))
    return jnp.where(side == 0, state, adjoint)


def solution(mesh):
    placed = (P("half", "gx", "yz", None), P("gx", "yz", None), P())
    return jax.shard_map(
        on_device,
        mesh=mesh,
        in_specs=placed,
        out_specs=P("half", "gx", "yz", None),
        check_vma=False,
    )
```

profile of v0, /device:TPU:12, one launch (start us, length us, event | category | flops | bytes accessed | tf_op | source)
XLA Modules:
  0.0 424.3 jit_solution(2569210067173966610)
XLA Ops:
  7.0 2.4 collective-permute-start.2
  9.3 3.5 collective-permute-start.3
  15.1 2.2 select_maximum_fusion.40
  17.4 4.0 fusion.82
  22.7 3.7 collective-permute-start.5
  27.4 1.9 collective-permute-start.6
  29.3 3.9 collective-permute-start.7
  35.1 3.7 select_maximum_fusion.36
  38.8 4.5 %fusion.74 = f32[1,64,64,128]{3,2,1,0:T(8,128)S(1)} fusion(f32[1,64,64,128]{3,2,1,0:T(8,128)S(1)} %fusion.82, f32[1,66,66,130]{3,2,1,0:T(8,128)S(1)} %select_maximum_fusion.36, f32[1,66,1,128]{3,2,1,0:T(1,128)S(1)} %collective-permute-done.7, f32[1,1,64,128]{3,2,1,0:T(8,128)S(1)} %collective-permute-done.4, ...), kind=kLoop, calls=%fused_computation.186 | loop fusion | flops 13107200 | bytes 10618884 | tf_op jit(solution)/shard_map/add | solution.py:50
  44.7 3.3 collective-permute-start.9
  48.9 1.9 collective-permute-start.10
  50.8 4.1 collective-permute-start.11
  56.6 3.7 select_maximum_fusion.32
  60.3 4.5 %fusion.66 = f32[1,64,64,128]{3,2,1,0:T(8,128)S(1)} fusion(f32[1,64,64,128]{3,2,1,0:T(8,128)S(1)} %fusion.74, f32[1,66,66,130]{3,2,1,0:T(8,128)S(1)} %select_maximum_fusion.32, f32[1,66,1,128]{3,2,1,0:T(1,128)S(1)} %collective-permute-done.11, f32[1,1,64,128]{3,2,1,0:T(8,128)S(1)} %collective-permute-done.8, ...), kind=kLoop, calls=%fused_computation.168 | loop fusion | flops 13107200 | bytes 10618884 | tf_op jit(solution)/shard_map/add | solution.py:50
  64.9 3.7 pad_maximum_fusion
  71.2 5.0 %collective-permute-start.13 = (f32[1,1,64,128]{3,2,1,0:T(8,128)S(1)}, f32[1,1,64,128]{3,2,1,0:T(8,128)S(1)}, u32[]{:S(2)}, u32[]{:S(2)}) collective-permute-start(f32[1,1,64,128]{3,2,1,0:T(8,128)S(1)} %get-tuple-element.37), channel_id=1, source_target_pairs={{0,4},{4,8},{8,12},{1,5},{5,9},{9,13},{2,6},{6,10},{10,14},{3,7},{... | collective-permute-start | bytes 98312 | tf_op jit(solution)/shard_map/ppermute | solution.py:18
  76.3 176.3 %collective-permute-done.16 = f32[4,1,64,64,128]{4,3,2,1,0:T(8,128)} collective-permute-done((f32[4,1,64,64,128]{4,3,2,1,0:T(8,128)}, f32[4,1,64,64,128]{4,3,2,1,0:T(8,128)}, u32[]{:S(2)}, u32[]{:S(2)}) %collective-permute-start.16) | collective-permute-done | bytes 8388640 | tf_op jit(solution)/shard_map/ppermute | solution.py:27
  252.6 4.3 %slice_bitcast_fusion = (f32[1,64,64,128]{3,2,1,0:T(8,128)S(1)}, f32[1,64,64,128]{3,2,1,0:T(8,128)S(1)}, f32[1,64,64,128]{3,2,1,0:T(8,128)S(1)}, f32[1,64,64,128]{3,2,1,0:T(8,128)S(1)}) fusion(f32[4,1,64,64,128]{4,3,2,1,0:T(8,128)} %collective-permute-done.16), kind=kLoop, calls=%fused_computation.77 | loop fusion | bytes 16777216 | tf_op jit(solution)/shard_map/squeeze | solution.py:82
  258.2 4.0 collective-permute-start.18
  264.3 2.2 collective-permute-start.20
  266.5 3.9 collective-permute-start.19
  271.8 4.9 %collective-permute-start.22 = (f32[1,1,64,128]{3,2,1,0:T(8,128)S(1)}, f32[1,1,64,128]{3,2,1,0:T(8,128)S(1)}, u32[]{:S(2)}, u32[]{:S(2)}) collective-permute-start(f32[1,1,64,128]{3,2,1,0:T(8,128)S(1)} %get-tuple-element.47), channel_id=1, source_target_pairs={{0,4},{4,8},{8,12},{1,5},{5,9},{9,13},{2,6},{6,10},{10,14},{3,7},{... | collective-permute-start | bytes 98312 | tf_op jit(solution)/shard_map/ppermute | solution.py:18
  276.7 7.5 %fusion.3 = f32[1,66,66,130]{3,2,1,0:T(8,128)} fusion(f32[1,66,1,128]{3,2,1,0:T(1,128)S(1)} %collective-permute-done.20, f32[1,66,1,128]{3,2,1,0:T(1,128)S(1)} %collective-permute-done.19, f32[1,1,64,128]{3,2,1,0:T(8,128)S(1)} %collective-permute-done.17, f32[1,64,64,128]{3,2,1,0:T(8,128)S(1)} %get-tuple-element.8, ...), kind=kLoop, calls=%fused_computation.31 | loop fusion | flops 10193040 | bytes 6725664 | tf_op jit(solution)/shard_map/mul | solution.py:63
  284.2 8.0 %fusion.49 = f32[1,64,64,128]{3,2,1,0:T(8,128)S(1)} fusion(f32[1,64,64,128]{3,2,1,0:T(8,128)S(1)} %copy-done.5, f32[1,66,66,130]{3,2,1,0:T(8,128)} %fusion.3, f32[1,64,64,128]{3,2,1,0:T(8,128)S(1)} %get-tuple-element.8, f32[1,1,64,128]{3,2,1,0:T(8,128)S(1)} %collective-permute-done.18, f32[1,1,64,128]{3,2,1,0:T(8,128)S(1)} %collective-permute-done.17, ...), kind=kLoop, calls=%fused_computation.137 | loop fusion | flops 12582912 | bytes 17041408 | tf_op jit(solution)/shard_map/add | solution.py:61
  293.5 4.4 %collective-permute-start.25 = (f32[1,1,64,128]{3,2,1,0:T(8,128)S(1)}, f32[1,1,64,128]{3,2,1,0:T(8,128)S(1)}, u32[]{:S(2)}, u32[]{:S(2)}) collective-permute-start(f32[1,1,64,128]{3,2,1,0:T(8,128)S(1)} %get-tuple-element.49), channel_id=1, source_target_pairs={{0,4},{4,8},{8,12},{1,5},{5,9},{9,13},{2,6},{6,10},{10,14},{3,7},{... | collective-permute-start | bytes 98312 | tf_op jit(solution)/shard_map/ppermute | solution.py:18
  299.1 1.9 collective-permute-start.24
  301.0 3.9 collective-permute-start.23
  306.9 3.9 collective-permute-start.27
  312.2 3.5 collective-permute-start.30
  315.7 8.9 %fusion.2 = (f32[1,66,66,130]{3,2,1,0:T(8,128)S(1)}, f32[1,66,66,130]{3,2,1,0:T(8,128)}) fusion(f32[1,66,1,128]{3,2,1,0:T(1,128)S(1)} %collective-permute-done.24, f32[1,66,1,128]{3,2,1,0:T(1,128)S(1)} %collective-permute-done.23, f32[1,1,64,128]{3,2,1,0:T(8,128)S(1)} %collective-permute-done.21, f32[1,64,64,128]{3,2,1,0:T(8,128)S(1)} %copy-done.8, ...), kind=kLoop, calls=%fused_computation.26 | loop fusion | flops 12458160 | bytes 8990784 | tf_op jit(solution)/shard_map/mul | solution.py:63
  324.6 8.0 %fusion.36 = f32[1,64,64,128]{3,2,1,0:T(8,128)S(1)} fusion(f32[1,64,64,128]{3,2,1,0:T(8,128)S(1)} %fusion.49, f32[1,66,66,130]{3,2,1,0:T(8,128)} %get-tuple-element.14, f32[1,66,1,128]{3,2,1,0:T(1,128)S(1)} %collective-permute-done.27, f32[1,1,64,128]{3,2,1,0:T(8,128)S(1)} %collective-permute-done.26, f32[1,1,64,128]{3,2,1,0:T(8,128)S(1)} %collective-permute-done.25, ...), kind=kLoop, calls=%fused_computation.110 | loop fusion | flops 14680064 | bytes 14878720 | tf_op jit(solution)/shard_map/add | solution.py:61
  333.9 4.3 %collective-permute-start.33 = (f32[1,1,64,128]{3,2,1,0:T(8,128)S(1)}, f32[1,1,64,128]{3,2,1,0:T(8,128)S(1)}, u32[]{:S(2)}, u32[]{:S(2)}) collective-permute-start(f32[1,1,64,128]{3,2,1,0:T(8,128)S(1)} %get-tuple-element.45), channel_id=1, source_target_pairs={{0,4},{4,8},{8,12},{1,5},{5,9},{9,13},{2,6},{6,10},{10,14},{3,7},{... | collective-permute-start | bytes 98312 | tf_op jit(solution)/shard_map/ppermute | solution.py:18
  338.3 2.2 collective-permute-start.32
  340.5 3.6 collective-permute-start.31
  344.2 2.2 collective-permute-start.36
  346.4 3.6 collective-permute-start.35
  350.1 3.6 collective-permute-start.15
  355.1 3.0 collective-permute-start.38
  358.1 7.7 %fusion.1 = (f32[1,66,66,130]{3,2,1,0:T(8,128)S(1)}, f32[1,66,66,130]{3,2,1,0:T(8,128)S(1)}) fusion(f32[1,66,1,128]{3,2,1,0:T(1,128)S(1)} %collective-permute-done.32, f32[1,66,1,128]{3,2,1,0:T(1,128)S(1)} %collective-permute-done.31, f32[1,1,64,128]{3,2,1,0:T(8,128)S(1)} %collective-permute-done.29, f32[1,64,64,128]{3,2,1,0:T(8,128)S(1)} %get-tuple-element.6, ...), kind=kLoop, calls=%fused_computation.17 | loop fusion | flops 12458160 | bytes 8990784 | tf_op jit(solution)/shard_map/mul | solution.py:63
  365.8 5.8 %fusion.23 = f32[1,64,64,128]{3,2,1,0:T(8,128)S(1)} fusion(f32[1,64,64,128]{3,2,1,0:T(8,128)S(1)} %fusion.36, f32[1,66,66,130]{3,2,1,0:T(8,128)S(1)} %get-tuple-element.12, f32[1,66,1,128]{3,2,1,0:T(1,128)S(1)} %collective-permute-done.35, f32[1,1,64,128]{3,2,1,0:T(8,128)S(1)} %collective-permute-done.34, f32[1,1,64,128]{3,2,1,0:T(8,128)S(1)} %collective-permute-done.33, ...), kind=kLoop, calls=%fused_computation.83 | loop fusion | flops 14680064 | bytes 14878720 | tf_op jit(solution)/shard_map/add | solution.py:61
  373.0 4.1 collective-permute-start.41
  377.2 2.2 collective-permute-start.40
  379.4 3.6 collective-permute-start.39
  383.1 2.2 collective-permute-start.44
  385.3 3.9 collective-permute-start.43
  389.2 5.1 %select_maximum_fusion.28 = f32[1,66,66,130]{3,2,1,0:T(8,128)} fusion(f32[1,66,1,128]{3,2,1,0:T(1,128)S(1)} %collective-permute-done.14, f32[1,66,1,128]{3,2,1,0:T(1,128)S(1)} %collective-permute-done.15, f32[1,1,64,128]{3,2,1,0:T(8,128)S(1)} %collective-permute-done.12, f32[1,64,64,128]{3,2,1,0:T(8,128)S(1)} %fusion.66, ...), kind=kLoop, calls=%fused_computation.35 | loop fusion | flops 6795360 | bytes 4495392 | tf_op jit(solution)/shard_map/concatenate | solution.py:20
  394.4 9.5 %fusion = (f32[1,66,66,130]{3,2,1,0:T(8,128)}, f32[1,66,66,130]{3,2,1,0:T(8,128)}) fusion(f32[1,66,1,128]{3,2,1,0:T(1,128)S(1)} %collective-permute-done.40, f32[1,66,1,128]{3,2,1,0:T(1,128)S(1)} %collective-permute-done.39, f32[1,1,64,128]{3,2,1,0:T(8,128)S(1)} %collective-permute-done.37, f32[1,64,64,128]{3,2,1,0:T(8,128)S(1)} %get-tuple-element.5, ...), kind=kLoop, calls=%fused_computation.8 | loop fusion | flops 12458160 | bytes 8990784 | tf_op jit(solution)/shard_map/mul | solution.py:63
  403.8 20.0 %fusion.10 = f32[1,64,64,128]{3,2,1,0:T(8,128)} fusion(f32[1,64,64,128]{3,2,1,0:T(8,128)} %copy-done.3, f32[1,66,66,130]{3,2,1,0:T(8,128)} %get-tuple-element.10, f32[1,66,1,128]{3,2,1,0:T(1,128)S(1)} %collective-permute-done.43, f32[1,1,64,128]{3,2,1,0:T(8,128)S(1)} %collective-permute-done.42, f32[1,1,64,128]{3,2,1,0:T(8,128)S(1)} %collective-permute-done.41, ...), kind=kLoop, calls=%fused_computation.56 | loop fusion | flops 28311552 | bytes 23400452 | tf_op jit(solution)/shard_map/jit(_where)/select_n | solution.py:90
  (109 shorter events, 33.4 us)
Async XLA Ops:
  0.8 3.0 collective-permute-start.1
  2.5 4.4 %collective-permute-start = (f32[1,1,64,128]{3,2,1,0:T(8,128)S(1)}, f32[1,1,64,128]{3,2,1,0:T(8,128)S(1)}, u32[]{:S(2)}, u32[]{:S(2)}) collective-permute-start(f32[1,1,64,128]{3,2,1,0:T(8,128)S(1)} %get-tuple-element.58), channel_id=1, source_target_pairs={{4,0},{8,4},{12,8},{5,1},{9,5},{13,9},{6,2},{10,6},{14,10},{7,3},{... | collective-permute-start | bytes 98312 | tf_op jit(solution)/shard_map/ppermute | solution.py:19
  7.0 6.6 %collective-permute-start.2 = (f32[1,66,1,128]{3,2,1,0:T(1,128)S(1)}, f32[1,66,1,128]{3,2,1,0:T(1,128)S(1)}, u32[]{:S(2)}, u32[]{:S(2)}) collective-permute-start(f32[1,66,1,128]{3,2,1,0:T(1,128)S(1)} %get-tuple-element.36), channel_id=1, source_target_pairs={{1,0},{2,1},{3,2},{5,4},{6,5},{7,6},{9,8},{10,9},{11,10},{13,12},{... | collective-permute-start | bytes 101384 | tf_op jit(solution)/shard_map/ppermute | solution.py:19
  9.3 5.8 %collective-permute-start.3 = (f32[1,66,1,128]{3,2,1,0:T(1,128)S(1)}, f32[1,66,1,128]{3,2,1,0:T(1,128)S(1)}, u32[]{:S(2)}, u32[]{:S(2)}) collective-permute-start(f32[1,66,1,128]{3,2,1,0:T(1,128)S(1)} %get-tuple-element.35), channel_id=1, source_target_pairs={{0,1},{1,2},{2,3},{4,5},{5,6},{6,7},{8,9},{9,10},{10,11},{12,13},{... | collective-permute-start | bytes 101384 | tf_op jit(solution)/shard_map/ppermute | solution.py:18
  21.4 5.0 %collective-permute-start.4 = (f32[1,1,64,128]{3,2,1,0:T(8,128)S(1)}, f32[1,1,64,128]{3,2,1,0:T(8,128)S(1)}, u32[]{:S(2)}, u32[]{:S(2)}) collective-permute-start(f32[1,1,64,128]{3,2,1,0:T(8,128)S(1)} %get-tuple-element.56), channel_id=1, source_target_pairs={{4,0},{8,4},{12,8},{5,1},{9,5},{13,9},{6,2},{10,6},{14,10},{7,3},{... | collective-permute-start | bytes 98312 | tf_op jit(solution)/shard_map/ppermute | solution.py:19
  22.7 4.6 %collective-permute-start.5 = (f32[1,1,64,128]{3,2,1,0:T(8,128)S(1)}, f32[1,1,64,128]{3,2,1,0:T(8,128)S(1)}, u32[]{:S(2)}, u32[]{:S(2)}) collective-permute-start(f32[1,1,64,128]{3,2,1,0:T(8,128)S(1)} %get-tuple-element.55), channel_id=1, source_target_pairs={{0,4},{4,8},{8,12},{1,5},{5,9},{9,13},{2,6},{6,10},{10,14},{3,7},{... | collective-permute-start | bytes 98312 | tf_op jit(solution)/shard_map/ppermute | solution.py:18
  27.4 5.9 %collective-permute-start.6 = (f32[1,66,1,128]{3,2,1,0:T(1,128)S(1)}, f32[1,66,1,128]{3,2,1,0:T(1,128)S(1)}, u32[]{:S(2)}, u32[]{:S(2)}) collective-permute-start(f32[1,66,1,128]{3,2,1,0:T(1,128)S(1)} %get-tuple-element.34), channel_id=1, source_target_pairs={{1,0},{2,1},{3,2},{5,4},{6,5},{7,6},{9,8},{10,9},{11,10},{13,12},{... | collective-permute-start | bytes 101384 | tf_op jit(solution)/shard_map/ppermute | solution.py:19
  29.3 5.8 %collective-permute-start.7 = (f32[1,66,1,128]{3,2,1,0:T(1,128)S(1)}, f32[1,66,1,128]{3,2,1,0:T(1,128)S(1)}, u32[]{:S(2)}, u32[]{:S(2)}) collective-permute-start(f32[1,66,1,128]{3,2,1,0:T(1,128)S(1)} %get-tuple-element.33), channel_id=1, source_target_pairs={{0,1},{1,2},{2,3},{4,5},{5,6},{6,7},{8,9},{9,10},{10,11},{12,13},{... | collective-permute-start | bytes 101384 | tf_op jit(solution)/shard_map/ppermute | solution.py:18
  43.4 4.6 %collective-permute-start.8 = (f32[1,1,64,128]{3,2,1,0:T(8,128)S(1)}, f32[1,1,64,128]{3,2,1,0:T(8,128)S(1)}, u32[]{:S(2)}, u32[]{:S(2)}) collective-permute-start(f32[1,1,64,128]{3,2,1,0:T(8,128)S(1)} %get-tuple-element.54), channel_id=1, source_target_pairs={{4,0},{8,4},{12,8},{5,1},{9,5},{13,9},{6,2},{10,6},{14,10},{7,3},{... | collective-permute-start | bytes 98312 | tf_op jit(solution)/shard_map/ppermute | solution.py:19
  44.7 4.1 collective-permute-start.9
  48.9 6.1 %collective-permute-start.10 = (f32[1,66,1,128]{3,2,1,0:T(1,128)S(1)}, f32[1,66,1,128]{3,2,1,0:T(1,128)S(1)}, u32[]{:S(2)}, u32[]{:S(2)}) collective-permute-start(f32[1,66,1,128]{3,2,1,0:T(1,128)S(1)} %get-tuple-element.32), channel_id=1, source_target_pairs={{1,0},{2,1},{3,2},{5,4},{6,5},{7,6},{9,8},{10,9},{11,10},{13,12},{... | collective-permute-start | bytes 101384 | tf_op jit(solution)/shard_map/ppermute | solution.py:19
  50.8 5.8 %collective-permute-start.11 = (f32[1,66,1,128]{3,2,1,0:T(1,128)S(1)}, f32[1,66,1,128]{3,2,1,0:T(1,128)S(1)}, u32[]{:S(2)}, u32[]{:S(2)}) collective-permute-start(f32[1,66,1,128]{3,2,1,0:T(1,128)S(1)} %get-tuple-element.31), channel_id=1, source_target_pairs={{0,1},{1,2},{2,3},{4,5},{5,6},{6,7},{8,9},{9,10},{10,11},{12,13},{... | collective-permute-start | bytes 101384 | tf_op jit(solution)/shard_map/ppermute | solution.py:18
  68.5 184.0 %collective-permute-start.16 = (f32[4,1,64,64,128]{4,3,2,1,0:T(8,128)}, f32[4,1,64,64,128]{4,3,2,1,0:T(8,128)}, u32[]{:S(2)}, u32[]{:S(2)}) collective-permute-start(f32[4,1,64,64,128]{4,3,2,1,0:T(8,128)} %pad_maximum_fusion), channel_id=1, source_target_pairs={{0,16},{1,17},{2,18},{3,19},{4,20},{5,21},{6,22},{7,23},{8,24},{9,... | collective-permute-start | bytes 25165832 | tf_op jit(solution)/shard_map/ppermute | solution.py:27
  69.9 192.3 %collective-permute-start.12 = (f32[1,1,64,128]{3,2,1,0:T(8,128)S(1)}, f32[1,1,64,128]{3,2,1,0:T(8,128)S(1)}, u32[]{:S(2)}, u32[]{:S(2)}) collective-permute-start(f32[1,1,64,128]{3,2,1,0:T(8,128)S(1)} %get-tuple-element.38), channel_id=1, source_target_pairs={{4,0},{8,4},{12,8},{5,1},{9,5},{13,9},{6,2},{10,6},{14,10},{7,3},{... | collective-permute-start | bytes 98312 | tf_op jit(solution)/shard_map/ppermute | solution.py:19
  71.2 191.0 %collective-permute-start.13 = (f32[1,1,64,128]{3,2,1,0:T(8,128)S(1)}, f32[1,1,64,128]{3,2,1,0:T(8,128)S(1)}, u32[]{:S(2)}, u32[]{:S(2)}) collective-permute-start(f32[1,1,64,128]{3,2,1,0:T(8,128)S(1)} %get-tuple-element.37), channel_id=1, source_target_pairs={{0,4},{4,8},{8,12},{1,5},{5,9},{9,13},{2,6},{6,10},{10,14},{3,7},{... | collective-permute-start | bytes 98312 | tf_op jit(solution)/shard_map/ppermute | solution.py:18
  256.9 137.5 %copy-start.6 = (f32[1,64,64,128]{3,2,1,0:T(8,128)}, f32[1,64,64,128]{3,2,1,0:T(8,128)S(1)}, u32[]{:S(2)}) copy-start(f32[1,64,64,128]{3,2,1,0:T(8,128)S(1)} %get-tuple-element.5) | copy-start | bytes 6291460
  256.9 7.3 %collective-permute-start.17 = (f32[1,1,64,128]{3,2,1,0:T(8,128)S(1)}, f32[1,1,64,128]{3,2,1,0:T(8,128)S(1)}, u32[]{:S(2)}, u32[]{:S(2)}) collective-permute-start(f32[1,1,64,128]{3,2,1,0:T(8,128)S(1)} %get-tuple-element.52), channel_id=1, source_target_pairs={{4,0},{8,4},{12,8},{5,1},{9,5},{13,9},{6,2},{10,6},{14,10},{7,3},{... | collective-permute-start | bytes 98312 | tf_op jit(solution)/shard_map/ppermute | solution.py:19
  258.2 6.0 %collective-permute-start.18 = (f32[1,1,64,128]{3,2,1,0:T(8,128)S(1)}, f32[1,1,64,128]{3,2,1,0:T(8,128)S(1)}, u32[]{:S(2)}, u32[]{:S(2)}) collective-permute-start(f32[1,1,64,128]{3,2,1,0:T(8,128)S(1)} %get-tuple-element.51), channel_id=1, source_target_pairs={{0,4},{4,8},{8,12},{1,5},{5,9},{9,13},{2,6},{6,10},{10,14},{3,7},{... | collective-permute-start | bytes 98312 | tf_op jit(solution)/shard_map/ppermute | solution.py:18
  262.3 123.0 %collective-permute-start.14 = (f32[1,66,1,128]{3,2,1,0:T(1,128)S(1)}, f32[1,66,1,128]{3,2,1,0:T(1,128)S(1)}, u32[]{:S(2)}, u32[]{:S(2)}) collective-permute-start(f32[1,66,1,128]{3,2,1,0:T(1,128)S(1)} %get-tuple-element.16), channel_id=1, source_target_pairs={{1,0},{2,1},{3,2},{5,4},{6,5},{7,6},{9,8},{10,9},{11,10},{13,12},{... | collective-permute-start | bytes 101384 | tf_op jit(solution)/shard_map/ppermute | solution.py:19
  264.3 12.4 %collective-permute-start.20 = (f32[1,66,1,128]{3,2,1,0:T(1,128)S(1)}, f32[1,66,1,128]{3,2,1,0:T(1,128)S(1)}, u32[]{:S(2)}, u32[]{:S(2)}) collective-permute-start(f32[1,66,1,128]{3,2,1,0:T(1,128)S(1)} %get-tuple-element.30), channel_id=1, source_target_pairs={{1,0},{2,1},{3,2},{5,4},{6,5},{7,6},{9,8},{10,9},{11,10},{13,12},{... | collective-permute-start | bytes 101384 | tf_op jit(solution)/shard_map/ppermute | solution.py:19
  266.5 10.2 %collective-permute-start.19 = (f32[1,66,1,128]{3,2,1,0:T(1,128)S(1)}, f32[1,66,1,128]{3,2,1,0:T(1,128)S(1)}, u32[]{:S(2)}, u32[]{:S(2)}) collective-permute-start(f32[1,66,1,128]{3,2,1,0:T(1,128)S(1)} %get-tuple-element.29), channel_id=1, source_target_pairs={{0,1},{1,2},{2,3},{4,5},{5,6},{6,7},{8,9},{9,10},{10,11},{12,13},{... | collective-permute-start | bytes 101384 | tf_op jit(solution)/shard_map/ppermute | solution.py:18
  270.5 27.5 %collective-permute-start.21 = (f32[1,1,64,128]{3,2,1,0:T(8,128)S(1)}, f32[1,1,64,128]{3,2,1,0:T(8,128)S(1)}, u32[]{:S(2)}, u32[]{:S(2)}) collective-permute-start(f32[1,1,64,128]{3,2,1,0:T(8,128)S(1)} %get-tuple-element.48), channel_id=1, source_target_pairs={{4,0},{8,4},{12,8},{5,1},{9,5},{13,9},{6,2},{10,6},{14,10},{7,3},{... | collective-permute-start | bytes 98312 | tf_op jit(solution)/shard_map/ppermute | solution.py:19
  271.8 26.2 %collective-permute-start.22 = (f32[1,1,64,128]{3,2,1,0:T(8,128)S(1)}, f32[1,1,64,128]{3,2,1,0:T(8,128)S(1)}, u32[]{:S(2)}, u32[]{:S(2)}) collective-permute-start(f32[1,1,64,128]{3,2,1,0:T(8,128)S(1)} %get-tuple-element.47), channel_id=1, source_target_pairs={{0,4},{4,8},{8,12},{1,5},{5,9},{9,13},{2,6},{6,10},{10,14},{3,7},{... | collective-permute-start | bytes 98312 | tf_op jit(solution)/shard_map/ppermute | solution.py:18
  292.2 12.7 %collective-permute-start.26 = (f32[1,1,64,128]{3,2,1,0:T(8,128)S(1)}, f32[1,1,64,128]{3,2,1,0:T(8,128)S(1)}, u32[]{:S(2)}, u32[]{:S(2)}) collective-permute-start(f32[1,1,64,128]{3,2,1,0:T(8,128)S(1)} %get-tuple-element.50), channel_id=1, source_target_pairs={{4,0},{8,4},{12,8},{5,1},{9,5},{13,9},{6,2},{10,6},{14,10},{7,3},{... | collective-permute-start | bytes 98312 | tf_op jit(solution)/shard_map/ppermute | solution.py:19
  293.5 22.2 %copy-start.8 = (f32[1,64,64,128]{3,2,1,0:T(8,128)S(1)}, f32[1,64,64,128]{3,2,1,0:T(8,128)}, u32[]{:S(2)}) copy-start(f32[1,64,64,128]{3,2,1,0:T(8,128)} %copy-done.7) | copy-start | bytes 6291460
  293.5 11.4 %collective-permute-start.25 = (f32[1,1,64,128]{3,2,1,0:T(8,128)S(1)}, f32[1,1,64,128]{3,2,1,0:T(8,128)S(1)}, u32[]{:S(2)}, u32[]{:S(2)}) collective-permute-start(f32[1,1,64,128]{3,2,1,0:T(8,128)S(1)} %get-tuple-element.49), channel_id=1, source_target_pairs={{0,4},{4,8},{8,12},{1,5},{5,9},{9,13},{2,6},{6,10},{10,14},{3,7},{... | collective-permute-start | bytes 98312 | tf_op jit(solution)/shard_map/ppermute | solution.py:18
  299.1 11.8 %collective-permute-start.24 = (f32[1,66,1,128]{3,2,1,0:T(1,128)S(1)}, f32[1,66,1,128]{3,2,1,0:T(1,128)S(1)}, u32[]{:S(2)}, u32[]{:S(2)}) collective-permute-start(f32[1,66,1,128]{3,2,1,0:T(1,128)S(1)} %get-tuple-element.26), channel_id=1, source_target_pairs={{1,0},{2,1},{3,2},{5,4},{6,5},{7,6},{9,8},{10,9},{11,10},{13,12},{... | collective-permute-start | bytes 101384 | tf_op jit(solution)/shard_map/ppermute | solution.py:19
  301.0 11.2 %collective-permute-start.23 = (f32[1,66,1,128]{3,2,1,0:T(1,128)S(1)}, f32[1,66,1,128]{3,2,1,0:T(1,128)S(1)}, u32[]{:S(2)}, u32[]{:S(2)}) collective-permute-start(f32[1,66,1,128]{3,2,1,0:T(1,128)S(1)} %get-tuple-element.25), channel_id=1, source_target_pairs={{0,1},{1,2},{2,3},{4,5},{5,6},{6,7},{8,9},{9,10},{10,11},{12,13},{... | collective-permute-start | bytes 101384 | tf_op jit(solution)/shard_map/ppermute | solution.py:18
  305.0 10.7 %collective-permute-start.28 = (f32[1,66,1,128]{3,2,1,0:T(1,128)S(1)}, f32[1,66,1,128]{3,2,1,0:T(1,128)S(1)}, u32[]{:S(2)}, u32[]{:S(2)}) collective-permute-start(f32[1,66,1,128]{3,2,1,0:T(1,128)S(1)} %get-tuple-element.28), channel_id=1, source_target_pairs={{1,0},{2,1},{3,2},{5,4},{6,5},{7,6},{9,8},{10,9},{11,10},{13,12},{... | collective-permute-start | bytes 101384 | tf_op jit(solution)/shard_map/ppermute | solution.py:19
  306.9 8.7 %collective-permute-start.27 = (f32[1,66,1,128]{3,2,1,0:T(1,128)S(1)}, f32[1,66,1,128]{3,2,1,0:T(1,128)S(1)}, u32[]{:S(2)}, u32[]{:S(2)}) collective-permute-start(f32[1,66,1,128]{3,2,1,0:T(1,128)S(1)} %get-tuple-element.27), channel_id=1, source_target_pairs={{0,1},{1,2},{2,3},{4,5},{5,6},{6,7},{8,9},{9,10},{10,11},{12,13},{... | collective-permute-start | bytes 101384 | tf_op jit(solution)/shard_map/ppermute | solution.py:18
  310.9 27.3 %collective-permute-start.29 = (f32[1,1,64,128]{3,2,1,0:T(8,128)S(1)}, f32[1,1,64,128]{3,2,1,0:T(8,128)S(1)}, u32[]{:S(2)}, u32[]{:S(2)}) collective-permute-start(f32[1,1,64,128]{3,2,1,0:T(8,128)S(1)} %get-tuple-element.44), channel_id=1, source_target_pairs={{4,0},{8,4},{12,8},{5,1},{9,5},{13,9},{6,2},{10,6},{14,10},{7,3},{... | collective-permute-start | bytes 98312 | tf_op jit(solution)/shard_map/ppermute | solution.py:19
  312.2 26.0 %collective-permute-start.30 = (f32[1,1,64,128]{3,2,1,0:T(8,128)S(1)}, f32[1,1,64,128]{3,2,1,0:T(8,128)S(1)}, u32[]{:S(2)}, u32[]{:S(2)}) collective-permute-start(f32[1,1,64,128]{3,2,1,0:T(8,128)S(1)} %get-tuple-element.43), channel_id=1, source_target_pairs={{0,4},{4,8},{8,12},{1,5},{5,9},{9,13},{2,6},{6,10},{10,14},{3,7},{... | collective-permute-start | bytes 98312 | tf_op jit(solution)/shard_map/ppermute | solution.py:18
  332.6 11.5 %collective-permute-start.34 = (f32[1,1,64,128]{3,2,1,0:T(8,128)S(1)}, f32[1,1,64,128]{3,2,1,0:T(8,128)S(1)}, u32[]{:S(2)}, u32[]{:S(2)}) collective-permute-start(f32[1,1,64,128]{3,2,1,0:T(8,128)S(1)} %get-tuple-element.46), channel_id=1, source_target_pairs={{4,0},{8,4},{12,8},{5,1},{9,5},{13,9},{6,2},{10,6},{14,10},{7,3},{... | collective-permute-start | bytes 98312 | tf_op jit(solution)/shard_map/ppermute | solution.py:19
  333.9 10.2 %collective-permute-start.33 = (f32[1,1,64,128]{3,2,1,0:T(8,128)S(1)}, f32[1,1,64,128]{3,2,1,0:T(8,128)S(1)}, u32[]{:S(2)}, u32[]{:S(2)}) collective-permute-start(f32[1,1,64,128]{3,2,1,0:T(8,128)S(1)} %get-tuple-element.45), channel_id=1, source_target_pairs={{0,4},{4,8},{8,12},{1,5},{5,9},{9,13},{2,6},{6,10},{10,14},{3,7},{... | collective-permute-start | bytes 98312 | tf_op jit(solution)/shard_map/ppermute | solution.py:18
  338.3 11.8 %collective-permute-start.32 = (f32[1,66,1,128]{3,2,1,0:T(1,128)S(1)}, f32[1,66,1,128]{3,2,1,0:T(1,128)S(1)}, u32[]{:S(2)}, u32[]{:S(2)}) collective-permute-start(f32[1,66,1,128]{3,2,1,0:T(1,128)S(1)} %get-tuple-element.22), channel_id=1, source_target_pairs={{1,0},{2,1},{3,2},{5,4},{6,5},{7,6},{9,8},{10,9},{11,10},{13,12},{... | collective-permute-start | bytes 101384 | tf_op jit(solution)/shard_map/ppermute | solution.py:19
  340.5 13.3 %collective-permute-start.31 = (f32[1,66,1,128]{3,2,1,0:T(1,128)S(1)}, f32[1,66,1,128]{3,2,1,0:T(1,128)S(1)}, u32[]{:S(2)}, u32[]{:S(2)}) collective-permute-start(f32[1,66,1,128]{3,2,1,0:T(1,128)S(1)} %get-tuple-element.21), channel_id=1, source_target_pairs={{0,1},{1,2},{2,3},{4,5},{5,6},{6,7},{8,9},{9,10},{10,11},{12,13},{... | collective-permute-start | bytes 101384 | tf_op jit(solution)/shard_map/ppermute | solution.py:18
  344.2 10.8 %collective-permute-start.36 = (f32[1,66,1,128]{3,2,1,0:T(1,128)S(1)}, f32[1,66,1,128]{3,2,1,0:T(1,128)S(1)}, u32[]{:S(2)}, u32[]{:S(2)}) collective-permute-start(f32[1,66,1,128]{3,2,1,0:T(1,128)S(1)} %get-tuple-element.24), channel_id=1, source_target_pairs={{1,0},{2,1},{3,2},{5,4},{6,5},{7,6},{9,8},{10,9},{11,10},{13,12},{... | collective-permute-start | bytes 101384 | tf_op jit(solution)/shard_map/ppermute | solution.py:19
  346.4 11.7 %collective-permute-start.35 = (f32[1,66,1,128]{3,2,1,0:T(1,128)S(1)}, f32[1,66,1,128]{3,2,1,0:T(1,128)S(1)}, u32[]{:S(2)}, u32[]{:S(2)}) collective-permute-start(f32[1,66,1,128]{3,2,1,0:T(1,128)S(1)} %get-tuple-element.23), channel_id=1, source_target_pairs={{0,1},{1,2},{2,3},{4,5},{5,6},{6,7},{8,9},{9,10},{10,11},{12,13},{... | collective-permute-start | bytes 101384 | tf_op jit(solution)/shard_map/ppermute | solution.py:18
  350.1 39.1 %collective-permute-start.15 = (f32[1,66,1,128]{3,2,1,0:T(1,128)S(1)}, f32[1,66,1,128]{3,2,1,0:T(1,128)S(1)}, u32[]{:S(2)}, u32[]{:S(2)}) collective-permute-start(f32[1,66,1,128]{3,2,1,0:T(1,128)S(1)} %get-tuple-element.15), channel_id=1, source_target_pairs={{0,1},{1,2},{2,3},{4,5},{5,6},{6,7},{8,9},{9,10},{10,11},{12,13},{... | collective-permute-start | bytes 101384 | tf_op jit(solution)/shard_map/ppermute | solution.py:18
  353.8 19.2 %collective-permute-start.37 = (f32[1,1,64,128]{3,2,1,0:T(8,128)S(1)}, f32[1,1,64,128]{3,2,1,0:T(8,128)S(1)}, u32[]{:S(2)}, u32[]{:S(2)}) collective-permute-start(f32[1,1,64,128]{3,2,1,0:T(8,128)S(1)} %get-tuple-element.40), channel_id=1, source_target_pairs={{4,0},{8,4},{12,8},{5,1},{9,5},{13,9},{6,2},{10,6},{14,10},{7,3},{... | collective-permute-start | bytes 98312 | tf_op jit(solution)/shard_map/ppermute | solution.py:19
  355.1 22.0 %collective-permute-start.38 = (f32[1,1,64,128]{3,2,1,0:T(8,128)S(1)}, f32[1,1,64,128]{3,2,1,0:T(8,128)S(1)}, u32[]{:S(2)}, u32[]{:S(2)}) collective-permute-start(f32[1,1,64,128]{3,2,1,0:T(8,128)S(1)} %get-tuple-element.39), channel_id=1, source_target_pairs={{0,4},{4,8},{8,12},{1,5},{5,9},{9,13},{2,6},{6,10},{10,14},{3,7},{... | collective-permute-start | bytes 98312 | tf_op jit(solution)/shard_map/ppermute | solution.py:18
  371.6 22.8 %copy-start.3 = (f32[1,64,64,128]{3,2,1,0:T(8,128)}, f32[1,64,64,128]{3,2,1,0:T(8,128)S(1)}, u32[]{:S(2)}) copy-start(f32[1,64,64,128]{3,2,1,0:T(8,128)S(1)} %fusion.23) | copy-start | bytes 6291460
  371.7 7.7 %collective-permute-start.42 = (f32[1,1,64,128]{3,2,1,0:T(8,128)S(1)}, f32[1,1,64,128]{3,2,1,0:T(8,128)S(1)}, u32[]{:S(2)}, u32[]{:S(2)}) collective-permute-start(f32[1,1,64,128]{3,2,1,0:T(8,128)S(1)} %get-tuple-element.42), channel_id=1, source_target_pairs={{4,0},{8,4},{12,8},{5,1},{9,5},{13,9},{6,2},{10,6},{14,10},{7,3},{... | collective-permute-start | bytes 98312 | tf_op jit(solution)/shard_map/ppermute | solution.py:19
  373.0 10.1 %collective-permute-start.41 = (f32[1,1,64,128]{3,2,1,0:T(8,128)S(1)}, f32[1,1,64,128]{3,2,1,0:T(8,128)S(1)}, u32[]{:S(2)}, u32[]{:S(2)}) collective-permute-start(f32[1,1,64,128]{3,2,1,0:T(8,128)S(1)} %get-tuple-element.41), channel_id=1, source_target_pairs={{0,4},{4,8},{8,12},{1,5},{5,9},{9,13},{2,6},{6,10},{10,14},{3,7},{... | collective-permute-start | bytes 98312 | tf_op jit(solution)/shard_map/ppermute | solution.py:18
  377.2 17.2 %collective-permute-start.40 = (f32[1,66,1,128]{3,2,1,0:T(1,128)S(1)}, f32[1,66,1,128]{3,2,1,0:T(1,128)S(1)}, u32[]{:S(2)}, u32[]{:S(2)}) collective-permute-start(f32[1,66,1,128]{3,2,1,0:T(1,128)S(1)} %get-tuple-element.18), channel_id=1, source_target_pairs={{1,0},{2,1},{3,2},{5,4},{6,5},{7,6},{9,8},{10,9},{11,10},{13,12},{... | collective-permute-start | bytes 101384 | tf_op jit(solution)/shard_map/ppermute | solution.py:19
  379.4 15.0 %collective-permute-start.39 = (f32[1,66,1,128]{3,2,1,0:T(1,128)S(1)}, f32[1,66,1,128]{3,2,1,0:T(1,128)S(1)}, u32[]{:S(2)}, u32[]{:S(2)}) collective-permute-start(f32[1,66,1,128]{3,2,1,0:T(1,128)S(1)} %get-tuple-element.17), channel_id=1, source_target_pairs={{0,1},{1,2},{2,3},{4,5},{5,6},{6,7},{8,9},{9,10},{10,11},{12,13},{... | collective-permute-start | bytes 101384 | tf_op jit(solution)/shard_map/ppermute | solution.py:18
  383.1 11.3 %collective-permute-start.44 = (f32[1,66,1,128]{3,2,1,0:T(1,128)S(1)}, f32[1,66,1,128]{3,2,1,0:T(1,128)S(1)}, u32[]{:S(2)}, u32[]{:S(2)}) collective-permute-start(f32[1,66,1,128]{3,2,1,0:T(1,128)S(1)} %get-tuple-element.20), channel_id=1, source_target_pairs={{1,0},{2,1},{3,2},{5,4},{6,5},{7,6},{9,8},{10,9},{11,10},{13,12},{... | collective-permute-start | bytes 101384 | tf_op jit(solution)/shard_map/ppermute | solution.py:19
  385.3 9.1 %collective-permute-start.43 = (f32[1,66,1,128]{3,2,1,0:T(1,128)S(1)}, f32[1,66,1,128]{3,2,1,0:T(1,128)S(1)}, u32[]{:S(2)}, u32[]{:S(2)}) collective-permute-start(f32[1,66,1,128]{3,2,1,0:T(1,128)S(1)} %get-tuple-element.19), channel_id=1, source_target_pairs={{0,1},{1,2},{2,3},{4,5},{5,6},{6,7},{8,9},{9,10},{10,11},{12,13},{... | collective-permute-start | bytes 101384 | tf_op jit(solution)/shard_map/ppermute | solution.py:18
  (9 other events, 99.2 us)
where the time goes:
time: 433 us; the launch traced here: 424 us
  waiting for transfers between devices  184 us (42%)
  starting transfers between devices  122 us (28%)
  other arithmetic  108 us (25%)
  local copies, waits for them, and re-layouts  7.01 us (2%)
    ppermute x1, waiting for transfers between devices, from_behind(): lax.ppermute(value, axis, [(source, source + steps) for source in range(l...  176 us
    ppermute x22, starting transfers between devices, padded_2(): before = lax.ppermute(last, axis, up)  83.6 us
    ppermute x22, starting transfers between devices, padded_2(): after = lax.ppermute(leading, axis, down)  37.2 us
    mul x4, other arithmetic, retreat(): padded_base * padded_adj  33.5 us
    add x3, other arithmetic, retreat(): adjoint + 0.2 * (-adjoint * along_x(padded_base) + along_x(padded_base *...  21.8 us
    select_n x1, other arithmetic, on_device(): return jnp.where(side == 0, state, adjoint)  20 us
    concatenate x7, other arithmetic, padded_2(): value = jnp.concatenate([before, value, after], axis=dim)  14.9 us
    add x3, other arithmetic, update(): field + 0.2 * (-field * along_x(padded) + 0.5 * laplace(padded) + forcing...  13 us
  transfers between devices with their start and end apart: 45, of which 7 were waited for; matrix products, arithmetic and copies ran while one was open for 14% of the time, Pallas kernels for 0%

commit v1 on v0

v1 whole, which is shorter than its diff:
```python
import functools
import math

import jax
import jax.numpy as jnp
from jax import lax
from jax.experimental import pallas as pl
from jax.experimental.pallas import tpu as pltpu
from jax.sharding import PartitionSpec as P

ITERS = 4
MESH = pl.DeviceIdType.MESH


def window(chunks, step_ref, fields, forcing, out, state, yh, sy, force, send, recv, base_send, base_recv, local):
    X, Y, Z = force.shape
    W = X // chunks
    order = [0, chunks - 1] + list(range(1, chunks - 1))
    side = lax.axis_index("half")
    gx, nx = lax.axis_index("gx"), lax.axis_size("gx")
    gy, ny = lax.axis_index("yz"), lax.axis_size("yz")
    has_left, has_right = gx > 0, gx < nx - 1
    has_down, has_up = gy > 0, gy < ny - 1
    left, right = {"gx": lax.rem(gx + nx - 1, nx)}, {"gx": lax.rem(gx + 1, nx)}
    down, up = {"yz": lax.rem(gy + ny - 1, ny)}, {"yz": lax.rem(gy + 1, ny)}
    other = {"half": 1 - side}

    def remote(src, dst, s, r, dev):
        return pltpu.make_async_remote_copy(
            src_ref=src, dst_ref=dst, send_sem=s, recv_sem=r, device_id=dev, device_id_type=MESH
        )

    def x_left(k):
        return remote(state.at[k, 1], state.at[k, X + 1], send.at[k, 0], recv.at[k, 0], left)

    def x_right(k):
        return remote(state.at[k, X], state.at[k, 0], send.at[k, 1], recv.at[k, 1], right)

    def y_down(k, c):
        part = pl.ds(c * W, W)
        return remote(sy.at[k, 0, part], yh.at[k, 1, part], send.at[k, 2 + c], recv.at[k, 2 + c], down)

    def y_up(k, c):
        part, s = pl.ds(c * W, W), 2 + chunks + c
        return remote(sy.at[k, 1, part], yh.at[k, 0, part], send.at[k, s], recv.at[k, s], up)

    def brick(c):
        return remote(
            fields.at[0, pl.ds(c * W, W)], state.at[0, pl.ds(1 + c * W, W)], base_send.at[c], base_recv.at[c], other
        )

    def send_chunk(k, c, along_y=True):
        if c == 0:
            pl.when(has_left)(lambda: x_left(k).start())
        if c == chunks - 1:
            pl.when(has_right)(lambda: x_right(k).start())
        if along_y:
            pl.when(has_down)(lambda: y_down(k, c).start())
            pl.when(has_up)(lambda: y_up(k, c).start())

    def recv_x(k, c):
        if c == 0:
            pl.when(has_left)(lambda: x_right(k).wait_recv())
        if c == chunks - 1:
            pl.when(has_right)(lambda: x_left(k).wait_recv())

    def recv_y(k, c):
        pl.when(has_up)(lambda: y_down(k, c).wait_recv())
        pl.when(has_down)(lambda: y_up(k, c).wait_recv())

    def sent(k, along_y=True):
        pl.when(has_left)(lambda: x_left(k).wait_send())
        pl.when(has_right)(lambda: x_right(k).wait_send())
        if along_y:
            for c in range(chunks):
                pl.when(has_down)(lambda: y_down(k, c).wait_send())
                pl.when(has_up)(lambda: y_up(k, c).wait_send())

    neighbours = ((has_left, left), (has_right, right), (has_down, down), (has_up, up))

    force_in = pltpu.make_async_copy(forcing, force, local.at[0])
    force_in.start()

    def own(k):
        return pltpu.make_async_copy(fields.at[0], state.at[k, pl.ds(1, X)], local.at[1])

    pl.when(side == 0)(lambda: own(0).start())
    pl.when(side == 1)(lambda: own(ITERS).start())

    barrier = pltpu.get_barrier_semaphore()
    pl.semaphore_signal(barrier, inc=1, device_id=other, device_id_type=MESH)
    for has, dev in neighbours:
        pl.when(has)(functools.partial(pl.semaphore_signal, barrier, inc=1, device_id=dev, device_id_type=MESH))
    sides = lax.div(gx + nx - 1, nx) + lax.div(2 * nx - 2 - gx, nx)
    sides = sides + lax.div(gy + ny - 1, ny) + lax.div(2 * ny - 2 - gy, ny)
    pl.semaphore_wait(barrier, 1 + sides)

    @pl.when(side == 0)
    def _():
        for c in order:
            brick(c).start()

    zero_plane = jnp.zeros((Y, Z), jnp.float32)
    zero_rows = jnp.zeros((X, Z), jnp.float32)
    for k in range(2 * ITERS):

        @pl.when(jnp.logical_not(has_left))
        def _():
            state[k, 0] = zero_plane

        @pl.when(jnp.logical_not(has_right))
        def _():
            state[k, X + 1] = zero_plane

        @pl.when(jnp.logical_not(has_down))
        def _():
            yh[k, 0] = zero_rows

        @pl.when(jnp.logical_not(has_up))
        def _():
            yh[k, 1] = zero_rows

    row = lax.broadcasted_iota(jnp.int32, (Y, Z), 0)
    lane = lax.broadcasted_iota(jnp.int32, (Y, Z), 1)

    def edge_rows(k, i, value):
        sy[k, 0, pl.ds(i, 1), :] = value[0:1]
        sy[k, 1, pl.ds(i, 1), :] = value[Y - 1 : Y]

    def edges_of(k, c):
        def one(i, carry):
            edge_rows(k, i, state[k, i + 1])
            return carry

        lax.fori_loop(c * W, (c + 1) * W, one, 0)

    def around(k, i, mid):
        below = jnp.where(row == 0, yh[k, 0, pl.ds(i, 1), :], pltpu.roll(mid, 1, 0))
        above = jnp.where(row == Y - 1, yh[k, 1, pl.ds(i, 1), :], pltpu.roll(mid, Y - 1, 0))
        before = jnp.where(lane == 0, 0.0, pltpu.roll(mid, 1, 1))
        after = jnp.where(lane == Z - 1, 0.0, pltpu.roll(mid, Z - 1, 1))
        return (below + above) + (before + after)

    def forward(k, c, last=False):
        phase = (step_ref[0] + k).astype(jnp.float32) * (2.0 * math.pi / 64.0)
        level = 0.2 * jnp.sin(jnp.full((1, Z), phase, jnp.float32))

        def one(i, carry):
            mid, prev, nxt = state[k, i + 1], state[k, i], state[k, i + 2]
            total = around(k, i, mid) + (nxt + prev) - mid * (nxt - prev)
            new = 0.4 * mid + 0.1 * total + force[i] * level
            if last:
                out[0, i] = new
            else:
                state[k + 1, i + 1] = new
                edge_rows(k + 1, i, new)
            return carry

        lax.fori_loop(c * W, (c + 1) * W, one, 0)

    def backward(k, b, c, last=False):
        def one(i, carry):
            mid, prev, nxt = state[k, i + 1], state[k, i], state[k, i + 2]
            total = around(k, i, mid) + (nxt + prev)
            total = total + state[b, i + 2] * (nxt - mid) - state[b, i] * (prev - mid)
            new = 0.4 * mid + 0.1 * total
            if last:
                out[0, i] = new
            else:
                state[k + 1, i + 1] = new
                edge_rows(k + 1, i, new)
            return carry

        lax.fori_loop(c * W, (c + 1) * W, one, 0)

    @pl.when(side == 0)
    def _():
        own(0).wait()
        for c in order:
            edges_of(0, c)
            send_chunk(0, c)

    @pl.when(side == 1)
    def _():
        own(ITERS).wait()
        for c in order:
            edges_of(ITERS, c)
            send_chunk(ITERS, c)
        for c in order:
            brick(c).wait_recv()
            edges_of(0, c)
            send_chunk(0, c)

    force_in.wait()
    for k in range(ITERS - 1):
        for c in order:
            recv_x(k, c)
            recv_y(k, c)
            forward(k, c)
            if k < ITERS - 2:
                send_chunk(k + 1, c)
            else:
                send_chunk(k + 1, c, along_y=False)

                @pl.when(side == 0)
                def _():
                    pl.when(has_down)(lambda: y_down(k + 1, c).start())
                    pl.when(has_up)(lambda: y_up(k + 1, c).start())

    @pl.when(side == 0)
    def _():
        k = ITERS - 1
        for c in order:
            recv_x(k, c)
            recv_y(k, c)
            forward(k, c, last=True)
        for k in range(ITERS):
            sent(k)
        for c in range(chunks):
            brick(c).wait_send()

    @pl.when(side == 1)
    def _():
        for m in range(ITERS):
            k, b = ITERS + m, ITERS - 1 - m
            for c in order:
                recv_x(k, c)
                recv_y(k, c)
                if m == 0:
                    recv_x(b, c)
                backward(k, b, c, last=m == ITERS - 1)
                if m < ITERS - 1:
                    send_chunk(k + 1, c)
        for k in range(2 * ITERS):
            sent(k, along_y=k != ITERS - 1)


def on_device(fields, forcing, step_index):
    X, Y, Z = forcing.shape
    chunks = 4
    levels = 2 * ITERS
    return pl.pallas_call(
        functools.partial(window, chunks),
        out_shape=jax.ShapeDtypeStruct(fields.shape, jnp.float32),
        in_specs=[
            pl.BlockSpec(memory_space=pltpu.SMEM),
            pl.BlockSpec(memory_space=pl.ANY),
            pl.BlockSpec(memory_space=pl.ANY),
        ],
        out_specs=pl.BlockSpec(memory_space=pltpu.VMEM),
        scratch_shapes=[
            pltpu.VMEM((levels, X + 2, Y, Z), jnp.float32),
            pltpu.VMEM((levels, 2, X, Z), jnp.float32),
            pltpu.VMEM((levels, 2, X, Z), jnp.float32),
            pltpu.VMEM((X, Y, Z), jnp.float32),
            pltpu.SemaphoreType.DMA((levels, 2 + 2 * chunks)),
            pltpu.SemaphoreType.DMA((levels, 2 + 2 * chunks)),
            pltpu.SemaphoreType.DMA((chunks,)),
            pltpu.SemaphoreType.DMA((chunks,)),
            pltpu.SemaphoreType.DMA((2,)),
        ],
        compiler_params=pltpu.CompilerParams(
            collective_id=0, has_side_effects=True, vmem_limit_bytes=56 * 1024 * 1024
        ),
        name="window",
    )(step_index, fields, forcing)


def solution(mesh):
    placed = (P("half", "gx", "yz", None), P("gx", "yz", None), P())
    return jax.shard_map(
        on_device,
        mesh=mesh,
        in_specs=placed,
        out_specs=P("half", "gx", "yz", None),
        check_vma=False,
    )
```

time: 433 us -> 97.8 us (0.23); the launches traced: 424 us -> 97.7 us
  waiting for transfers between devices: 184 us -> 0 us
  starting transfers between devices: 122 us -> 0 us
  other arithmetic: 108 us -> 0 us
  Pallas kernels: 0 us -> 93.9 us
    ppermute x45 -> x0, waiting for transfers between devices: 184 us -> none  [the longest x1 176 us: from_behind(): lax.ppermute(value, axis, [(source, source + steps) for source in range(l...]
    ppermute x45 -> x0, starting transfers between devices: 122 us -> none  [the longest x22 83.6 us: padded_2(): before = lax.ppermute(last, axis, up)]
    pallas_call x0 -> x1, Pallas kernels: none -> 93.9 us  [on_device(): pl.pallas_call(functools.partial(window, chunks), out_shape=jax.ShapeDtyp...]
    add x6 -> x0, other arithmetic: 34.8 us -> none  [the longest x3 21.8 us: retreat(): adjoint + 0.2 * (-adjoint * along_x(padded_base) + along_x(padded_base *...]
    mul x4 -> x0, other arithmetic: 33.5 us -> none  [retreat(): padded_base * padded_adj]
    select_n x1 -> x0, other arithmetic: 20 us -> none  [on_device(): return jnp.where(side == 0, state, adjoint)]
    concatenate x7 -> x0, other arithmetic: 14.9 us -> none  [padded_2(): value = jnp.concatenate([before, value, after], axis=dim)]
  transfers between devices with their start and end apart: 45 -> 0, of which waited for: 7 -> 0; matrix products, arithmetic and copies ran while one was open for 14% -> 0% of each run, Pallas kernels for 0% -> 0%
where the time goes in v1:
time: 97.8 us; the launch traced here: 97.7 us
  Pallas kernels  93.9 us (96%)
  local copies, waits for them, and re-layouts  3.16 us (3%)
    pallas_call x1, Pallas kernels, on_device(): pl.pallas_call(functools.partial(window, chunks), out_shape=jax.ShapeDtyp...  93.9 us
    unnamed x1, local copies, waits for them, and re-layouts  3.16 us

profile of v1, /device:TPU:12, one launch (start us, length us, event | category | flops | bytes accessed | tf_op | source)
XLA Modules:
  0.0 97.7 jit_solution(16791634633281001925)
XLA Ops:
  0.7 93.9 %window.1 = f32[1,64,64,128]{3,2,1,0:T(8,128)} custom-call(s32[1]{0:T(128)S(6)} %copy.5.step_ref, f32[1,64,64,128]{3,2,1,0:T(8,128)} %fields.1, f32[64,64,128]{2,1,0:T(8,128)} %forcing.1), custom_call_target="tpu_custom_call" | custom-call | tf_op jit(solution)/shard_map/window/pallas_call | solution.py:242
  94.5 3.2 %copy.6 = f32[1,64,64,128]{3,2,1,0:T(8,128)} copy(f32[1,64,64,128]{3,2,1,0:T(8,128)} %window.1) | data formatting | bytes 4194304

commit v2 on v1

v2 whole, which is shorter than its diff:
```python
import functools
import math

import jax
import jax.numpy as jnp
from jax import lax
from jax.experimental import pallas as pl
from jax.experimental.pallas import tpu as pltpu
from jax.sharding import PartitionSpec as P

ITERS = 4
MESH = pl.DeviceIdType.MESH


def window(chunks, step_ref, fields, forcing, out, state, yh, sy, force, send, recv, base_send, base_recv, local):
    X, Y, Z = force.shape
    W = X // chunks
    side = lax.axis_index("half")
    gx, nx = lax.axis_index("gx"), lax.axis_size("gx")
    gy, ny = lax.axis_index("yz"), lax.axis_size("yz")
    has_left, has_right = gx > 0, gx < nx - 1
    has_down, has_up = gy > 0, gy < ny - 1
    left, right = {"gx": lax.rem(gx + nx - 1, nx)}, {"gx": lax.rem(gx + 1, nx)}
    down, up = {"yz": lax.rem(gy + ny - 1, ny)}, {"yz": lax.rem(gy + 1, ny)}
    other = {"half": 1 - side}
    odd = lax.rem(gx, 2)
    near = {"gx": lax.rem(gx + nx - 1 + 2 * odd, nx)}
    far = {"gx": lax.rem(gx + nx + 1 - 2 * odd, nx)}
    has_near = jnp.logical_or(jnp.logical_and(odd == 0, has_left), jnp.logical_and(odd == 1, has_right))
    has_far = jnp.logical_or(jnp.logical_and(odd == 0, has_right), jnp.logical_and(odd == 1, has_left))

    def first(p):
        return (p + odd * (chunks - 1 - 2 * p)) * W

    def remote(src, dst, s, r, dev):
        return pltpu.make_async_remote_copy(
            src_ref=src, dst_ref=dst, send_sem=s, recv_sem=r, device_id=dev, device_id_type=MESH
        )

    def x_near(k):
        dst = (1 - odd) * (X + 1)
        return remote(state.at[k, 1 + odd * (X - 1)], state.at[k, dst], send.at[k, 0], recv.at[k, 0], near)

    def x_far(k):
        dst = odd * (X + 1)
        return remote(state.at[k, X - odd * (X - 1)], state.at[k, dst], send.at[k, 1], recv.at[k, 1], far)

    def y_down(k, p):
        part, s = pl.ds(first(p), W), 2 + p
        return remote(sy.at[k, 0, part], yh.at[k, 1, part], send.at[k, s], recv.at[k, s], down)

    def y_up(k, p):
        part, s = pl.ds(first(p), W), 2 + chunks + p
        return remote(sy.at[k, 1, part], yh.at[k, 0, part], send.at[k, s], recv.at[k, s], up)

    def brick(p):
        src, dst = fields.at[0, pl.ds(first(p), W)], state.at[0, pl.ds(1 + first(p), W)]
        return remote(src, dst, base_send.at[p], base_recv.at[p], other)

    def send_chunk(k, p, along_y=True):
        pl.when(jnp.logical_and(p == 0, has_near))(lambda: x_near(k).start())
        pl.when(jnp.logical_and(p == chunks - 1, has_far))(lambda: x_far(k).start())
        if along_y:
            pl.when(has_down)(lambda: y_down(k, p).start())
            pl.when(has_up)(lambda: y_up(k, p).start())

    def recv_x(k, p):
        pl.when(jnp.logical_and(p == 0, has_near))(lambda: x_near(k).wait_recv())
        pl.when(jnp.logical_and(p == chunks - 1, has_far))(lambda: x_far(k).wait_recv())

    def recv_y(k, p):
        pl.when(has_up)(lambda: y_down(k, p).wait_recv())
        pl.when(has_down)(lambda: y_up(k, p).wait_recv())

    def sent(k, along_y=True):
        pl.when(has_near)(lambda: x_near(k).wait_send())
        pl.when(has_far)(lambda: x_far(k).wait_send())
        if along_y:

            @pl.loop(0, chunks)
            def _(p):
                pl.when(has_down)(lambda: y_down(k, p).wait_send())
                pl.when(has_up)(lambda: y_up(k, p).wait_send())

    neighbours = ((has_left, left), (has_right, right), (has_down, down), (has_up, up))

    force_in = pltpu.make_async_copy(forcing, force, local.at[0])
    force_in.start()

    def own(k):
        return pltpu.make_async_copy(fields.at[0], state.at[k, pl.ds(1, X)], local.at[1])

    pl.when(side == 0)(lambda: own(0).start())
    pl.when(side == 1)(lambda: own(ITERS).start())

    barrier = pltpu.get_barrier_semaphore()
    pl.semaphore_signal(barrier, inc=1, device_id=other, device_id_type=MESH)
    for has, dev in neighbours:
        pl.when(has)(functools.partial(pl.semaphore_signal, barrier, inc=1, device_id=dev, device_id_type=MESH))
    sides = lax.div(gx + nx - 1, nx) + lax.div(2 * nx - 2 - gx, nx)
    sides = sides + lax.div(gy + ny - 1, ny) + lax.div(2 * ny - 2 - gy, ny)
    pl.semaphore_wait(barrier, 1 + sides)

    @pl.when(side == 0)
    def _():
        @pl.loop(0, chunks)
        def _(p):
            brick(p).start()

    zero_plane = jnp.zeros((Y, Z), jnp.float32)
    zero_rows = jnp.zeros((X, Z), jnp.float32)
    for k in range(2 * ITERS):

        @pl.when(jnp.logical_not(has_left))
        def _():
            state[k, 0] = zero_plane

        @pl.when(jnp.logical_not(has_right))
        def _():
            state[k, X + 1] = zero_plane

        @pl.when(jnp.logical_not(has_down))
        def _():
            yh[k, 0] = zero_rows

        @pl.when(jnp.logical_not(has_up))
        def _():
            yh[k, 1] = zero_rows

    row = lax.broadcasted_iota(jnp.int32, (Y, Z), 0)
    lane = lax.broadcasted_iota(jnp.int32, (Y, Z), 1)

    def edge_rows(k, i, value):
        sy[k, 0, pl.ds(i, 1), :] = value[0:1]
        sy[k, 1, pl.ds(i, 1), :] = value[Y - 1 : Y]

    def edges_of(k, p):
        for j in range(W):
            i = first(p) + j
            edge_rows(k, i, state[k, i + 1])

    def around(k, i, mid):
        below = jnp.where(row == 0, yh[k, 0, pl.ds(i, 1), :], pltpu.roll(mid, 1, 0))
        above = jnp.where(row == Y - 1, yh[k, 1, pl.ds(i, 1), :], pltpu.roll(mid, Y - 1, 0))
        before = jnp.where(lane == 0, 0.0, pltpu.roll(mid, 1, 1))
        after = jnp.where(lane == Z - 1, 0.0, pltpu.roll(mid, Z - 1, 1))
        return (below + above) + (before + after)

    def forward(k, p, last=False):
        phase = (step_ref[0] + k).astype(jnp.float32) * (2.0 * math.pi / 64.0)
        level = 0.2 * jnp.sin(jnp.full((1, Z), phase, jnp.float32))
        for j in range(W):
            i = first(p) + j
            mid, prev, nxt = state[k, i + 1], state[k, i], state[k, i + 2]
            total = around(k, i, mid) + (nxt + prev) - mid * (nxt - prev)
            new = 0.4 * mid + 0.1 * total + force[i] * level
            if last:
                out[0, i] = new
            else:
                state[k + 1, i + 1] = new
                edge_rows(k + 1, i, new)

    def backward(k, b, p, last=False):
        for j in range(W):
            i = first(p) + j
            mid, prev, nxt = state[k, i + 1], state[k, i], state[k, i + 2]
            total = around(k, i, mid) + (nxt + prev)
            total = total + state[b, i + 2] * (nxt - mid) - state[b, i] * (prev - mid)
            new = 0.4 * mid + 0.1 * total
            if last:
                out[0, i] = new
            else:
                state[k + 1, i + 1] = new
                edge_rows(k + 1, i, new)

    def task(t, lag, run):
        p = t - lag
        pl.when(jnp.logical_and(p >= 0, p < chunks))(functools.partial(run, p))

    def step_base(k, last_needed, p):
        recv_x(k, p)
        recv_y(k, p)
        forward(k, p, last=k == ITERS - 1)
        if k < ITERS - 1:
            send_chunk(k + 1, p, along_y=k + 1 < last_needed)

    def step_adjoint(m, p):
        k, b = ITERS + m, ITERS - 1 - m
        recv_x(k, p)
        recv_y(k, p)
        if m == 0:
            recv_x(b, p)
        backward(k, b, p, last=m == ITERS - 1)
        if m < ITERS - 1:
            send_chunk(k + 1, p)

    force_in.wait()

    @pl.when(side == 0)
    def _():
        own(0).wait()

        def begin(p):
            edges_of(0, p)
            send_chunk(0, p)

        @pl.loop(0, chunks + ITERS)
        def _(t):
            task(t, 0, begin)
            for k in range(ITERS):
                task(t, 1 + k, functools.partial(step_base, k, ITERS))

        for k in range(ITERS):
            sent(k)

        @pl.loop(0, chunks)
        def _(p):
            brick(p).wait_send()

    @pl.when(side == 1)
    def _():
        own(ITERS).wait()

        @pl.loop(0, chunks)
        def _(p):
            edges_of(ITERS, p)
            send_chunk(ITERS, p)

        def begin(p):
            brick(p).wait_recv()
            edges_of(0, p)
            send_chunk(0, p)

        @pl.loop(0, chunks + 2 * ITERS - 1)
        def _(t):
            task(t, 0, begin)
            for k in range(ITERS - 1):
                task(t, 1 + k, functools.partial(step_base, k, ITERS - 1))
            for m in range(ITERS):
                task(t, ITERS + m, functools.partial(step_adjoint, m))

        for k in range(2 * ITERS):
            sent(k, along_y=k != ITERS - 1)


def on_device(fields, forcing, step_index):
    X, Y, Z = forcing.shape
    chunks = 16
    levels = 2 * ITERS
    return pl.pallas_call(
        functools.partial(window, chunks),
        out_shape=jax.ShapeDtypeStruct(fields.shape, jnp.float32),
        in_specs=[
            pl.BlockSpec(memory_space=pltpu.SMEM),
            pl.BlockSpec(memory_space=pl.ANY),
            pl.BlockSpec(memory_space=pl.ANY),
        ],
        out_specs=pl.BlockSpec(memory_space=pltpu.VMEM),
        scratch_shapes=[
            pltpu.VMEM((levels, X + 2, Y, Z), jnp.float32),
            pltpu.VMEM((levels, 2, X, Z), jnp.float32),
            pltpu.VMEM((levels, 2, X, Z), jnp.float32),
            pltpu.VMEM((X, Y, Z), jnp.float32),
            pltpu.SemaphoreType.DMA((levels, 2 + 2 * chunks)),
            pltpu.SemaphoreType.DMA((levels, 2 + 2 * chunks)),
            pltpu.SemaphoreType.DMA((chunks,)),
            pltpu.SemaphoreType.DMA((chunks,)),
            pltpu.SemaphoreType.DMA((2,)),
        ],
        compiler_params=pltpu.CompilerParams(
            collective_id=0, has_side_effects=True, vmem_limit_bytes=56 * 1024 * 1024
        ),
        name="window",
    )(step_index, fields, forcing)


def solution(mesh):
    placed = (P("half", "gx", "yz", None), P("gx", "yz", None), P())
    return jax.shard_map(
        on_device,
        mesh=mesh,
        in_specs=placed,
        out_specs=P("half", "gx", "yz", None),
        check_vma=False,
    )
```

time: 97.8 us -> 78.9 us (0.81)
  Pallas kernels: 93.9 us -> 74.1 us
    pallas_call x1, Pallas kernels: 93.9 us -> 74.1 us  [on_device(): pl.pallas_call(functools.partial(window, chunks), out_shape=jax.ShapeDtyp...]
where the time goes in v2:
time: 78.9 us; the launch traced here: 77.9 us
  Pallas kernels  74.1 us (94%)
  local copies, waits for them, and re-layouts  3.16 us (4%)
    pallas_call x1, Pallas kernels, on_device(): pl.pallas_call(functools.partial(window, chunks), out_shape=jax.ShapeDtyp...  74.1 us
    unnamed x1, local copies, waits for them, and re-layouts  3.16 us

profile of v2, /device:TPU:12, one launch (start us, length us, event | category | flops | bytes accessed | tf_op | source)
XLA Modules:
  0.0 77.9 jit_solution(2539795937490715375)
XLA Ops:
  0.7 74.1 %window.1 = f32[1,64,64,128]{3,2,1,0:T(8,128)} custom-call(s32[1]{0:T(128)S(6)} %copy.5.step_ref, f32[1,64,64,128]{3,2,1,0:T(8,128)} %fields.1, f32[64,64,128]{2,1,0:T(8,128)} %forcing.1), custom_call_target="tpu_custom_call" | custom-call | tf_op jit(solution)/shard_map/window/pallas_call | solution.py:250
  74.7 3.2 %copy.6 = f32[1,64,64,128]{3,2,1,0:T(8,128)} copy(f32[1,64,64,128]{3,2,1,0:T(8,128)} %window.1) | data formatting | bytes 4194304

commit v3 on v2

--- a/solution.py
+++ b/solution.py
@@ -12,7 +12,7 @@
 MESH = pl.DeviceIdType.MESH
 
 
-def window(chunks, step_ref, fields, forcing, out, state, yh, sy, force, send, recv, base_send, base_recv, local):
+def window(chunks, cut, step_ref, fields, forcing, out, state, yh, sy, force, send, recv, base_send, base_recv, local):
     X, Y, Z = force.shape
     W = X // chunks
     side = lax.axis_index("half")
@@ -57,6 +57,14 @@
         src, dst = fields.at[0, pl.ds(first(p), W)], state.at[0, pl.ds(1 + first(p), W)]
         return remote(src, dst, base_send.at[p], base_recv.at[p], other)
 
+    def lent(p):
+        src, dst = fields.at[0, pl.ds(first(p), W)], state.at[ITERS, pl.ds(1 + first(p), W)]
+        return remote(src, dst, base_send.at[chunks + p], base_recv.at[chunks + p], other)
+
+    def returned(p):
+        src, dst = state.at[2 * ITERS, pl.ds(1 + first(p), W)], out.at[0, pl.ds(first(p), W)]
+        return remote(src, dst, base_send.at[2 * chunks + p], base_recv.at[2 * chunks + p], other)
+
     def send_chunk(k, p, along_y=True):
         pl.when(jnp.logical_and(p == 0, has_near))(lambda: x_near(k).start())
         pl.when(jnp.logical_and(p == chunks - 1, has_far))(lambda: x_far(k).start())
@@ -72,15 +80,17 @@
         pl.when(has_up)(lambda: y_down(k, p).wait_recv())
         pl.when(has_down)(lambda: y_up(k, p).wait_recv())
 
-    def sent(k, along_y=True):
-        pl.when(has_near)(lambda: x_near(k).wait_send())
-        pl.when(has_far)(lambda: x_far(k).wait_send())
-        if along_y:
-
-            @pl.loop(0, chunks)
-            def _(p):
-                pl.when(has_down)(lambda: y_down(k, p).wait_send())
-                pl.when(has_up)(lambda: y_up(k, p).wait_send())
+    def sent(k, lo, hi):
+        if lo == 0:
+            pl.when(has_near)(lambda: x_near(k).wait_send())
+        if hi == chunks:
+            pl.when(has_far)(lambda: x_far(k).wait_send())
+
+    def sent_y(k, lo, hi):
+        @pl.loop(lo, hi)
+        def _(p):
+            pl.when(has_down)(lambda: y_down(k, p).wait_send())
+            pl.when(has_up)(lambda: y_up(k, p).wait_send())
 
     neighbours = ((has_left, left), (has_right, right), (has_down, down), (has_up, up))
 
@@ -103,9 +113,15 @@
 
     @pl.when(side == 0)
     def _():
-        @pl.loop(0, chunks)
+        @pl.loop(0, cut + 2)
         def _(p):
             brick(p).start()
+
+    @pl.when(side == 1)
+    def _():
+        @pl.loop(cut - 1, chunks)
+        def _(p):
+            lent(p).start()
 
     zero_plane = jnp.zeros((Y, Z), jnp.float32)
     zero_rows = jnp.zeros((X, Z), jnp.float32)
@@ -160,7 +176,7 @@
                 state[k + 1, i + 1] = new
                 edge_rows(k + 1, i, new)
 
-    def backward(k, b, p, last=False):
+    def backward(k, b, p, last):
         for j in range(W):
             i = first(p) + j
             mid, prev, nxt = state[k, i + 1], state[k, i], state[k, i + 2]
@@ -171,11 +187,12 @@
                 out[0, i] = new
             else:
                 state[k + 1, i + 1] = new
-                edge_rows(k + 1, i, new)
-
-    def task(t, lag, run):
+                if k + 1 < 2 * ITERS:
+                    edge_rows(k + 1, i, new)
+
+    def task(t, lag, run, lo, hi):
         p = t - lag
-        pl.when(jnp.logical_and(p >= 0, p < chunks))(functools.partial(run, p))
+        pl.when(jnp.logical_and(p >= lo, p < hi))(functools.partial(run, p))
 
     def step_base(k, last_needed, p):
         recv_x(k, p)
@@ -184,15 +201,19 @@
         if k < ITERS - 1:
             send_chunk(k + 1, p, along_y=k + 1 < last_needed)
 
-    def step_adjoint(m, p):
+    def step_adjoint(m, p, home, lo, hi):
         k, b = ITERS + m, ITERS - 1 - m
         recv_x(k, p)
         recv_y(k, p)
-        if m == 0:
+        if m == 0 and home:
             recv_x(b, p)
-        backward(k, b, p, last=m == ITERS - 1)
-        if m < ITERS - 1:
+        backward(k, b, p, home and m == ITERS - 1)
+        if m == ITERS - 1 and not home:
+            returned(p).start()
+        if m < ITERS - 2:
             send_chunk(k + 1, p)
+        if m == ITERS - 2:
+            pl.when(jnp.logical_and(p >= lo, p < hi))(lambda: send_chunk(k + 1, p))
 
     force_in.wait()
 
@@ -204,24 +225,41 @@
             edges_of(0, p)
             send_chunk(0, p)
 
-        @pl.loop(0, chunks + ITERS)
+        def borrow(p):
+            lent(p).wait_recv()
+            edges_of(ITERS, p)
+            send_chunk(ITERS, p)
+
+        @pl.loop(0, chunks + 2 * ITERS - 1)
         def _(t):
-            task(t, 0, begin)
+            task(t, 0, begin, 0, chunks)
             for k in range(ITERS):
-                task(t, 1 + k, functools.partial(step_base, k, ITERS))
+                task(t, 1 + k, functools.partial(step_base, k, ITERS), 0, chunks)
+            task(t, ITERS - 1, borrow, cut - 1, chunks)
+            for m in range(ITERS):
+                run = functools.partial(step_adjoint, m, home=False, lo=cut, hi=chunks)
+                task(t, ITERS + m, run, cut if m == ITERS - 1 else cut - 1, chunks)
 
         for k in range(ITERS):
-            sent(k)
-
-        @pl.loop(0, chunks)
+            sent(k, 0, chunks)
+            sent_y(k, 0, chunks)
+        for k in range(ITERS, 2 * ITERS):
+            sent(k, cut, chunks)
+            sent_y(k, cut if k == 2 * ITERS - 1 else cut - 1, chunks)
+
+        @pl.loop(0, cut + 2)
         def _(p):
             brick(p).wait_send()
+
+        @pl.loop(cut, chunks)
+        def _(p):
+            returned(p).wait_send()
 
     @pl.when(side == 1)
     def _():
         own(ITERS).wait()
 
-        @pl.loop(0, chunks)
+        @pl.loop(0, cut + 1)
         def _(p):
             edges_of(ITERS, p)
             send_chunk(ITERS, p)
@@ -231,24 +269,38 @@
             edges_of(0, p)
             send_chunk(0, p)
 
-        @pl.loop(0, chunks + 2 * ITERS - 1)
+        @pl.loop(0, cut + 2 * ITERS)
         def _(t):
-            task(t, 0, begin)
+            task(t, 0, begin, 0, cut + 2)
             for k in range(ITERS - 1):
-                task(t, 1 + k, functools.partial(step_base, k, ITERS - 1))
+                task(t, 1 + k, functools.partial(step_base, k, ITERS - 1), 0, cut + 2)
             for m in range(ITERS):
-                task(t, ITERS + m, functools.partial(step_adjoint, m))
+                run = functools.partial(step_adjoint, m, home=True, lo=0, hi=cut)
+                task(t, ITERS + m, run, 0, cut if m == ITERS - 1 else cut + 1)
 
         for k in range(2 * ITERS):
-            sent(k, along_y=k != ITERS - 1)
+            sent(k, 0, cut)
+        for k in range(ITERS - 1):
+            sent_y(k, 0, cut + 2)
+        for k in range(ITERS, 2 * ITERS):
+            sent_y(k, 0, cut if k == 2 * ITERS - 1 else cut + 1)
+
+        @pl.loop(cut - 1, chunks)
+        def _(p):
+            lent(p).wait_send()
+
+        @pl.loop(cut, chunks)
+        def _(p):
+            returned(p).wait_recv()
 
 
 def on_device(fields, forcing, step_index):
     X, Y, Z = forcing.shape
     chunks = 16
+    cut = 5 * chunks // 8
     levels = 2 * ITERS
     return pl.pallas_call(
-        functools.partial(window, chunks),
+        functools.partial(window, chunks, cut),
         out_shape=jax.ShapeDtypeStruct(fields.shape, jnp.float32),
         in_specs=[
             pl.BlockSpec(memory_space=pltpu.SMEM),
@@ -257,14 +309,14 @@
         ],
         out_specs=pl.BlockSpec(memory_space=pltpu.VMEM),
         scratch_shapes=[
-            pltpu.VMEM((levels, X + 2, Y, Z), jnp.float32),
+            pltpu.VMEM((levels + 1, X + 2, Y, Z), jnp.float32),
             pltpu.VMEM((levels, 2, X, Z), jnp.float32),
             pltpu.VMEM((levels, 2, X, Z), jnp.float32),
             pltpu.VMEM((X, Y, Z), jnp.float32),
             pltpu.SemaphoreType.DMA((levels, 2 + 2 * chunks)),
             pltpu.SemaphoreType.DMA((levels, 2 + 2 * chunks)),
-            pltpu.SemaphoreType.DMA((chunks,)),
-            pltpu.SemaphoreType.DMA((chunks,)),
+            pltpu.SemaphoreType.DMA((3 * chunks,)),
+            pltpu.SemaphoreType.DMA((3 * chunks,)),
             pltpu.SemaphoreType.DMA((2,)),
         ],
         compiler_params=pltpu.CompilerParams(

time: 78.9 us -> 73.3 us (0.929)
  Pallas kernels: 74.1 us -> 68.5 us
    pallas_call x1, Pallas kernels: 74.1 us -> 68.5 us  [on_device(): pl.pallas_call(functools.partial(window, chunks, cut), out_shape=jax.Shap...]
where the time goes in v3:
time: 73.3 us; the launch traced here: 72.3 us
  Pallas kernels  68.5 us (93%)
  local copies, waits for them, and re-layouts  3.16 us (4%)
    pallas_call x1, Pallas kernels, on_device(): pl.pallas_call(functools.partial(window, chunks, cut), out_shape=jax.Shap...  68.5 us
    unnamed x1, local copies, waits for them, and re-layouts  3.16 us

profile of v3, /device:TPU:12, one launch (start us, length us, event | category | flops | bytes accessed | tf_op | source)
XLA Modules:
  0.0 72.3 jit_solution(10358230629660073527)
XLA Ops:
  0.7 68.5 %window.1 = f32[1,64,64,128]{3,2,1,0:T(8,128)} custom-call(s32[1]{0:T(128)S(6)} %copy.5.step_ref, f32[1,64,64,128]{3,2,1,0:T(8,128)} %fields.1, f32[64,64,128]{2,1,0:T(8,128)} %forcing.1), custom_call_target="tpu_custom_call" | custom-call | tf_op jit(solution)/shard_map/window/pallas_call | solution.py:302
  69.2 3.2 %copy.6 = f32[1,64,64,128]{3,2,1,0:T(8,128)} copy(f32[1,64,64,128]{3,2,1,0:T(8,128)} %window.1) | data formatting | bytes 4194304

commit v4 on v3

--- a/solution.py
+++ b/solution.py
@@ -23,7 +23,7 @@
     left, right = {"gx": lax.rem(gx + nx - 1, nx)}, {"gx": lax.rem(gx + 1, nx)}
     down, up = {"yz": lax.rem(gy + ny - 1, ny)}, {"yz": lax.rem(gy + 1, ny)}
     other = {"half": 1 - side}
-    odd = lax.rem(gx, 2)
+    parity, odd = lax.rem(gx, 2), lax.rem(gx + 1 - side, 2)
     near = {"gx": lax.rem(gx + nx - 1 + 2 * odd, nx)}
     far = {"gx": lax.rem(gx + nx + 1 - 2 * odd, nx)}
     has_near = jnp.logical_or(jnp.logical_and(odd == 0, has_left), jnp.logical_and(odd == 1, has_right))
@@ -32,6 +32,9 @@
     def first(p):
         return (p + odd * (chunks - 1 - 2 * p)) * W
 
+    def crossing(p):
+        return (p + parity * (chunks - 1 - 2 * p)) * W
+
     def remote(src, dst, s, r, dev):
         return pltpu.make_async_remote_copy(
             src_ref=src, dst_ref=dst, send_sem=s, recv_sem=r, device_id=dev, device_id_type=MESH
@@ -54,15 +57,15 @@
         return remote(sy.at[k, 1, part], yh.at[k, 0, part], send.at[k, s], recv.at[k, s], up)
 
     def brick(p):
-        src, dst = fields.at[0, pl.ds(first(p), W)], state.at[0, pl.ds(1 + first(p), W)]
+        src, dst = fields.at[0, pl.ds(crossing(p), W)], state.at[0, pl.ds(1 + crossing(p), W)]
         return remote(src, dst, base_send.at[p], base_recv.at[p], other)
 
     def lent(p):
-        src, dst = fields.at[0, pl.ds(first(p), W)], state.at[ITERS, pl.ds(1 + first(p), W)]
+        src, dst = fields.at[0, pl.ds(crossing(p), W)], state.at[ITERS, pl.ds(1 + crossing(p), W)]
         return remote(src, dst, base_send.at[chunks + p], base_recv.at[chunks + p], other)
 
     def returned(p):
-        src, dst = state.at[2 * ITERS, pl.ds(1 + first(p), W)], out.at[0, pl.ds(first(p), W)]
+        src, dst = state.at[2 * ITERS, pl.ds(1 + crossing(p), W)], out.at[0, pl.ds(crossing(p), W)]
         return remote(src, dst, base_send.at[2 * chunks + p], base_recv.at[2 * chunks + p], other)
 
     def send_chunk(k, p, along_y=True):
@@ -119,9 +122,9 @@
 
     @pl.when(side == 1)
     def _():
-        @pl.loop(cut - 1, chunks)
-        def _(p):
-            lent(p).start()
+        @pl.loop(0, chunks - cut + 1)
+        def _(p):
+            lent(chunks - 1 - p).start()
 
     zero_plane = jnp.zeros((Y, Z), jnp.float32)
     zero_rows = jnp.zeros((X, Z), jnp.float32)
@@ -209,7 +212,7 @@
             recv_x(b, p)
         backward(k, b, p, home and m == ITERS - 1)
         if m == ITERS - 1 and not home:
-            returned(p).start()
+            returned(chunks - 1 - p).start()
         if m < ITERS - 2:
             send_chunk(k + 1, p)
         if m == ITERS - 2:
@@ -225,27 +228,29 @@
             edges_of(0, p)
             send_chunk(0, p)
 
+        rest = chunks - cut
+
         def borrow(p):
-            lent(p).wait_recv()
+            lent(chunks - 1 - p).wait_recv()
             edges_of(ITERS, p)
             send_chunk(ITERS, p)
 
-        @pl.loop(0, chunks + 2 * ITERS - 1)
+        @pl.loop(0, chunks + ITERS)
         def _(t):
             task(t, 0, begin, 0, chunks)
             for k in range(ITERS):
                 task(t, 1 + k, functools.partial(step_base, k, ITERS), 0, chunks)
-            task(t, ITERS - 1, borrow, cut - 1, chunks)
+            task(t, ITERS - 1, borrow, 0, rest + 1)
             for m in range(ITERS):
-                run = functools.partial(step_adjoint, m, home=False, lo=cut, hi=chunks)
-                task(t, ITERS + m, run, cut if m == ITERS - 1 else cut - 1, chunks)
+                run = functools.partial(step_adjoint, m, home=False, lo=0, hi=rest)
+                task(t, ITERS + m, run, 0, rest if m == ITERS - 1 else rest + 1)
 
         for k in range(ITERS):
             sent(k, 0, chunks)
             sent_y(k, 0, chunks)
         for k in range(ITERS, 2 * ITERS):
-            sent(k, cut, chunks)
-            sent_y(k, cut if k == 2 * ITERS - 1 else cut - 1, chunks)
+            sent(k, 0, rest)
+            sent_y(k, 0, rest if k == 2 * ITERS - 1 else rest + 1)
 
         @pl.loop(0, cut + 2)
         def _(p):
@@ -297,7 +302,7 @@
 def on_device(fields, forcing, step_index):
     X, Y, Z = forcing.shape
     chunks = 16
-    cut = 5 * chunks // 8
+    cut = 9 * chunks // 16
     levels = 2 * ITERS
     return pl.pallas_call(
         functools.partial(window, chunks, cut),

time: 73.3 us -> 65.4 us (0.89)
  Pallas kernels: 68.5 us -> 60.9 us
    pallas_call x1, Pallas kernels: 68.5 us -> 60.9 us  [on_device(): pl.pallas_call(functools.partial(window, chunks, cut), out_shape=jax.Shap...]
where the time goes in v4:
time: 65.4 us; the launch traced here: 64.7 us
  Pallas kernels  60.9 us (93%)
  local copies, waits for them, and re-layouts  3.16 us (5%)
  between operations  0.66 us (1%)
    pallas_call x1, Pallas kernels, on_device(): pl.pallas_call(functools.partial(window, chunks, cut), out_shape=jax.Shap...  60.9 us
    unnamed x1, local copies, waits for them, and re-layouts  3.16 us

profile of v4, /device:TPU:12, one launch (start us, length us, event | category | flops | bytes accessed | tf_op | source)
XLA Modules:
  0.0 64.7 jit_solution(3510996062054248429)
XLA Ops:
  0.7 60.9 %window.1 = f32[1,64,64,128]{3,2,1,0:T(8,128)} custom-call(s32[1]{0:T(128)S(6)} %copy.5.step_ref, f32[1,64,64,128]{3,2,1,0:T(8,128)} %fields.1, f32[64,64,128]{2,1,0:T(8,128)} %forcing.1), custom_call_target="tpu_custom_call" | custom-call | tf_op jit(solution)/shard_map/window/pallas_call | solution.py:307
  61.6 3.2 %copy.6 = f32[1,64,64,128]{3,2,1,0:T(8,128)} copy(f32[1,64,64,128]{3,2,1,0:T(8,128)} %window.1) | data formatting | bytes 4194304

commit v5 on v4

--- a/solution.py
+++ b/solution.py
@@ -60,6 +60,11 @@
         src, dst = fields.at[0, pl.ds(crossing(p), W)], state.at[0, pl.ds(1 + crossing(p), W)]
         return remote(src, dst, base_send.at[p], base_recv.at[p], other)
 
+    def brick_end():
+        p, at = cut + 1, crossing(cut + 1) + parity
+        src, dst = fields.at[0, pl.ds(at, W - 1)], state.at[0, pl.ds(1 + at, W - 1)]
+        return remote(src, dst, base_send.at[p], base_recv.at[p], other)
+
     def lent(p):
         src, dst = fields.at[0, pl.ds(crossing(p), W)], state.at[ITERS, pl.ds(1 + crossing(p), W)]
         return remote(src, dst, base_send.at[chunks + p], base_recv.at[chunks + p], other)
@@ -116,9 +121,11 @@
 
     @pl.when(side == 0)
     def _():
-        @pl.loop(0, cut + 2)
+        @pl.loop(0, cut + 1)
         def _(p):
             brick(p).start()
+
+        brick_end().start()
 
     @pl.when(side == 1)
     def _():
@@ -252,9 +259,11 @@
             sent(k, 0, rest)
             sent_y(k, 0, rest if k == 2 * ITERS - 1 else rest + 1)
 
-        @pl.loop(0, cut + 2)
+        @pl.loop(0, cut + 1)
         def _(p):
             brick(p).wait_send()
+
+        brick_end().wait_send()
 
         @pl.loop(cut, chunks)
         def _(p):
@@ -270,7 +279,8 @@
             send_chunk(ITERS, p)
 
         def begin(p):
-            brick(p).wait_recv()
+            pl.when(p <= cut)(lambda: brick(p).wait_recv())
+            pl.when(p == cut + 1)(lambda: brick_end().wait_recv())
             edges_of(0, p)
             send_chunk(0, p)
 
@@ -302,7 +312,7 @@
 def on_device(fields, forcing, step_index):
     X, Y, Z = forcing.shape
     chunks = 16
-    cut = 9 * chunks // 16
+    cut = 5 * chunks // 8
     levels = 2 * ITERS
     return pl.pallas_call(
         functools.partial(window, chunks, cut),

time: 65.4 us -> 64.7 us (0.989)
  no operation moved by 1% of the time
where the time goes in v5:
time: 64.7 us; the launch traced here: 64.1 us
  Pallas kernels  60.3 us (93%)
  local copies, waits for them, and re-layouts  3.16 us (5%)
  between operations  0.66 us (1%)
    pallas_call x1, Pallas kernels, on_device(): pl.pallas_call(functools.partial(window, chunks, cut), out_shape=jax.Shap...  60.3 us
    unnamed x1, local copies, waits for them, and re-layouts  3.16 us

profile of v5, /device:TPU:12, one launch (start us, length us, event | category | flops | bytes accessed | tf_op | source)
XLA Modules:
  0.0 64.1 jit_solution(10861459276546587386)
XLA Ops:
  0.7 60.3 %window.1 = f32[1,64,64,128]{3,2,1,0:T(8,128)} custom-call(s32[1]{0:T(128)S(6)} %copy.5.step_ref, f32[1,64,64,128]{3,2,1,0:T(8,128)} %fields.1, f32[64,64,128]{2,1,0:T(8,128)} %forcing.1), custom_call_target="tpu_custom_call" | custom-call | tf_op jit(solution)/shard_map/window/pallas_call | solution.py:317
  61.0 3.2 %copy.6 = f32[1,64,64,128]{3,2,1,0:T(8,128)} copy(f32[1,64,64,128]{3,2,1,0:T(8,128)} %window.1) | data formatting | bytes 4194304
